TPU v7x, 32 devices: a whole 2x2x4 slice. The times are simulated.
32 devices in a mesh: blk: 8 (over z, x), rep: 4 (over y, core).
Axes of the slice: x: 2, y: 2, z: 4, core: 2. Of those that a mesh axis runs over, the one named last changes fastest.
Arguments:
- features: bfloat16 [32768, 128], P('blk'), may hold values from -6 to 6
- weight: bfloat16 [128, 256], replicated, may hold values from -0.5 to 0.5
- bias: float32 [256], replicated, may hold values from -3 to 3
- tile_values: bfloat16 [8, 8, 160, 128, 128], P('blk', 'rep'), may hold values from 0 to 0.041748047
- tile_place: int32 [8, 8, 160], P('blk', 'rep'), may hold values from 0 to 1023, as said below
- tile_count: int32 [8, 8], P('blk', 'rep'), may hold values from 1 to 160, as said below
Outputs:
- activations: bfloat16 [32768, 256], P('blk')
Inputs may be any that keep to these rules, and one draw needn't show every extreme that they name: `tile_place`: within one pair of destination block and section the 160 positions are distinct. `tile_count`: some pair of destination block and section has all 160 slots occupied.
All inputs are finite; a program needn't handle non-finite values.
Results may differ from a plain program's by a relative error of at most 0.0046.
Values may be sent and summed in bfloat16 or wider, within the bound.
A program may use at most 128 MiB of HBM per device.

v0:
```python
import jax
import jax.numpy as jnp
from jax import lax
from jax.sharding import PartitionSpec as P

TILE = 128


def section_terms(source, tiles, place, count):
    row_count = source.shape[0]
    row_tiles = row_count // TILE
    column = place % row_tiles
    target = place // row_tiles
    blocked = source.reshape(row_tiles, TILE, source.shape[1])
    pieces = jnp.take(blocked, column, axis=0)
    products = jnp.einsum("kij,kjf->kif", tiles, pieces, preferred_element_type=jnp.float32)
    slot_ids = jnp.arange(place.shape[0], dtype=jnp.int32)
    live = (slot_ids < count).astype(jnp.float32)
    products = products * live[:, None, None]
    summed = jax.ops.segment_sum(products, target, num_segments=row_tiles)
    return summed.reshape(row_count, source.shape[1])


def shards(features, weight, bias, tile_values, tile_place, tile_count):
    row_count = features.shape[0]
    sections = tile_values.shape[1]
    cycle_size = lax.axis_size("blk")
    my_replica = lax.axis_index("rep")
    partial_value = jnp.zeros((row_count, features.shape[1]), jnp.float32)
    piece_rows = row_count // cycle_size
    pieces = features.reshape(cycle_size, piece_rows, features.shape[1])
    holding = lax.all_to_all(pieces, "blk", split_axis=0, concat_axis=0, tiled=True)
    for section_index in range(sections):
        offset = my_replica * sections + section_index
        rolled = jnp.roll(holding, offset, axis=0)
        arrived = lax.all_to_all(rolled, "blk", split_axis=0, concat_axis=0, tiled=True)
        source = arrived.reshape(row_count, features.shape[1])
        partial_value = partial_value + section_terms(
            source,
            tile_values[0, section_index],
            tile_place[0, section_index],
            tile_count[0, section_index],
        )
    summed = lax.psum(partial_value, "rep")
    aggregated = summed.astype(jnp.bfloat16)
    output = jnp.dot(aggregated, weight, preferred_element_type=jnp.float32) + bias
    return jnp.maximum(output, 0.0).astype(jnp.bfloat16)


def solution(mesh):
    in_specs = (
        P("blk", None),
        P(),
        P(),
        P("blk", "rep", None, None, None),
        P("blk", "rep", None),
        P("blk", "rep"),
    )
    out_specs = P("blk", None)
    return jax.shard_map(shards, mesh=mesh, in_specs=in_specs, out_specs=out_specs, check_vma=False)
```

profile of v0, /device:TPU:1, one launch (start us, length us, event | category | flops | bytes accessed | tf_op | source)
XLA Modules:
  0.0 222.3 jit_solution(2415213686946378558)
XLA Ops:
  0.0 6.5 %all-to-all-start = ((bf16[8,512,128]{2,1,0:T(8,128)(2,1)}), bf16[8,512,128]{2,1,0:T(8,128)(2,1)S(1)}, u32[]{:S(2)}, u32[]{:S(2)}) async-start(bf16[8,512,128]{2,1,0:T(8,128)(2,1)} %bitcast.45), calls=%async_computation | async-start | bytes 2097152 | tf_op jit(solution)/shard_map/all_to_all | solution.py:32
  6.5 25.0 %all-to-all-done = bf16[8,512,128]{2,1,0:T(8,128)(2,1)S(1)} async-done(((bf16[8,512,128]{2,1,0:T(8,128)(2,1)}), bf16[8,512,128]{2,1,0:T(8,128)(2,1)S(1)}, u32[]{:S(2)}, u32[]{:S(2)}) %all-to-all-start) | async-done | bytes 1048608 | tf_op jit(solution)/shard_map/all_to_all | solution.py:32
  31.4 0.1 constant_dynamic-update-slice_fusion.1
  31.5 0.1 constant_dynamic-update-slice_fusion
  31.7 1.1 constant_dynamic-slice_fusion
  32.8 29.1 %all_to_all.15 = bf16[8,512,128]{2,1,0:T(8,128)(2,1)S(1)} all-to-all(bf16[8,512,128]{2,1,0:T(8,128)(2,1)S(1)} %get-tuple-element.11), channel_id=1, replica_groups=mesh['blk'=8,'rep'=4] {'blk'}, dimensions={0} | all-to-all | bytes 2097152 | tf_op jit(solution)/shard_map/all_to_all | solution.py:36
  61.9 4.3 %all-to-all-start.1 = ((bf16[8,512,128]{2,1,0:T(8,128)(2,1)}), bf16[8,512,128]{2,1,0:T(8,128)(2,1)S(1)}, u32[]{:S(2)}, u32[]{:S(2)}) async-start(bf16[8,512,128]{2,1,0:T(8,128)(2,1)} %get-tuple-element.12), calls=%async_computation.1 | async-start | bytes 2097152 | tf_op jit(solution)/shard_map/all_to_all | solution.py:36
  66.2 0.7 fusion.28
  66.9 0.7 compare_and_fusion
  67.6 0.6 compare_and_fusion.1
  68.2 7.7 %gather_fusion.1 = bf16[160,128,128]{2,1,0:T(8,128)(2,1)} fusion(bf16[32,128,128]{2,1,0:T(8,128)(2,1)S(1)} %bitcast.43, s32[1024]{0:T(1024)S(1)} %pad_clamp_fusion), kind=kCustom, calls=%fused_computation.1.clone | custom fusion | bytes 10486400 | tf_op jit(solution)/shard_map/jit(_take)/gather | solution.py:15
  75.9 11.8 %multiply_bitcast_fusion = f32[160,128,128]{1,2,0:T(8,128)} fusion(f32[160]{0:T(256)S(1)} %get-tuple-element.20, bf16[1,2,160,128,128]{4,3,2,1,0:T(8,128)(2,1)} %param.13, bf16[160,128,128]{2,1,0:T(8,128)(2,1)} %gather_fusion.1, pred[160]{0:T(512)(128)(4,1)S(1)} %get-tuple-element.6), kind=kOutput, calls=%fused_computation.4 | convolution fusion | flops 676331520 | bytes 20972320 | tf_op jit(solution)/shard_map/kij,kjf->kif/dot_general | solution.py:16
  87.7 11.7 %copy.12 = f32[160,128,128]{2,1,0:T(8,128)} copy(f32[160,128,128]{1,2,0:T(8,128)} %multiply_bitcast_fusion) | data formatting | bytes 20971520 | tf_op jit(solution)/shard_map/mul | solution.py:19
  99.5 7.7 %gather_fusion = bf16[160,128,128]{2,1,0:T(8,128)(2,1)} fusion(bf16[32,128,128]{2,1,0:T(8,128)(2,1)S(1)} %bitcast.42, s32[1024]{0:T(1024)S(1)} %pad_clamp_fusion.1), kind=kCustom, calls=%fused_computation.clone | custom fusion | bytes 10486400 | tf_op jit(solution)/shard_map/jit(_take)/gather | solution.py:15
  107.2 11.8 %multiply_bitcast_fusion.1 = f32[160,128,128]{1,2,0:T(8,128)} fusion(f32[160]{0:T(256)S(1)} %get-tuple-element.19, bf16[1,2,160,128,128]{4,3,2,1,0:T(8,128)(2,1)} %param.13, bf16[160,128,128]{2,1,0:T(8,128)(2,1)} %gather_fusion, pred[160]{0:T(512)(128)(4,1)S(1)} %get-tuple-element.9), kind=kOutput, calls=%fused_computation.5 | convolution fusion | flops 676331520 | bytes 20972320 | tf_op jit(solution)/shard_map/kij,kjf->kif/dot_general | solution.py:16
  119.0 11.7 %copy.10 = f32[160,128,128]{2,1,0:T(8,128)} copy(f32[160,128,128]{1,2,0:T(8,128)} %multiply_bitcast_fusion.1) | data formatting | bytes 20971520 | tf_op jit(solution)/shard_map/mul | solution.py:19
  130.7 0.2 broadcast.127.clone.1
  131.0 21.2 %scatter_fusion.1 = f32[32,128,128]{2,1,0:T(8,128)S(1)} fusion(f32[32,128,128]{2,1,0:T(8,128)S(1)} %broadcast.127.clone.1, s32[160]{0:T(256)S(1)} %bitcast.47, f32[160,128,128]{2,1,0:T(8,128)} %copy.12), kind=kCustom, calls=%fused_computation.3 | custom fusion | flops 2621440 | bytes 31457920 | tf_op jit(solution)/shard_map/scatter-add | solution.py:20
  152.2 1.3 copy-done.1
  153.5 0.2 broadcast.127.clone
  153.7 21.2 %scatter_fusion = f32[32,128,128]{2,1,0:T(8,128)S(1)} fusion(f32[32,128,128]{2,1,0:T(8,128)S(1)} %broadcast.127.clone, s32[160]{0:T(256)S(1)} %bitcast.46, f32[160,128,128]{2,1,0:T(8,128)} %copy.10), kind=kCustom, calls=%fused_computation.2 | custom fusion | flops 2621440 | bytes 31457920 | tf_op jit(solution)/shard_map/scatter-add | solution.py:20
  174.9 3.2 %add.66 = f32[32,128,128]{2,1,0:T(8,128)} add(f32[32,128,128]{2,1,0:T(8,128)S(1)} %scatter_fusion, f32[32,128,128]{2,1,0:T(8,128)} %copy-done.1) | non-fusion elementwise | flops 524288 | bytes 6291456 | tf_op jit(solution)/shard_map/add | solution.py:38
  178.1 42.2 %all-reduce.1 = bf16[4096,128]{1,0:T(8,128)(2,1)S(1)} all-reduce(f32[4096,128]{1,0:T(8,128)} %bitcast.44), channel_id=1, replica_groups=mesh['blk'=8,'rep'=4] {'rep'}, use_global_device_ids=true, to_apply=%region_2.5 | all-reduce | flops 524288 | bytes 3145728 | tf_op jit(solution)/shard_map/psum | solution.py:44
  220.3 2.0 fusion.11
  (14 shorter events, 0.1 us)
Async XLA Ops:
  0.0 220.3 %copy-start = (bf16[128,256]{1,0:T(8,128)(2,1)S(1)}, bf16[128,256]{1,0:T(8,128)(2,1)}, u32[]{:S(2)}) copy-start(bf16[128,256]{1,0:T(8,128)(2,1)} %param.11) | copy-start | bytes 196612
  0.0 31.4 %all-to-all-start = ((bf16[8,512,128]{2,1,0:T(8,128)(2,1)}), bf16[8,512,128]{2,1,0:T(8,128)(2,1)S(1)}, u32[]{:S(2)}, u32[]{:S(2)}) async-start(bf16[8,512,128]{2,1,0:T(8,128)(2,1)} %bitcast.45), calls=%async_computation | async-start | bytes 2097152 | tf_op jit(solution)/shard_map/all_to_all | solution.py:32
  31.5 34.7 %copy-start.2 = (s32[1,2,160]{2,1,0:T(2,128)S(1)}, s32[1,2,160]{2,1,0:T(2,128)}, u32[]{:S(2)}) copy-start(s32[1,2,160]{2,1,0:T(2,128)} %param.14) | copy-start | bytes 3844
  31.5 34.7 %copy-start.3 = (s32[1,2]{1,0:T(1,128)S(1)}, s32[1,2]{1,0:T(1,128)}, u32[]{:S(2)}) copy-start(s32[1,2]{1,0:T(1,128)} %param.15) | copy-start | bytes 28
  61.9 37.5 %all-to-all-start.1 = ((bf16[8,512,128]{2,1,0:T(8,128)(2,1)}), bf16[8,512,128]{2,1,0:T(8,128)(2,1)S(1)}, u32[]{:S(2)}, u32[]{:S(2)}) async-start(bf16[8,512,128]{2,1,0:T(8,128)(2,1)} %get-tuple-element.12), calls=%async_computation.1 | async-start | bytes 2097152 | tf_op jit(solution)/shard_map/all_to_all | solution.py:36
  152.2 1.3 copy-start.1
  174.9 45.4 %copy-start.4 = (f32[256]{0:T(256)S(1)}, f32[256]{0:T(256)}, u32[]{:S(2)}) copy-start(f32[256]{0:T(256)} %param.12) | copy-start | bytes 3076
where the time goes:
time: 224 us; the launch traced here: 222 us
  blocking collectives  71.3 us (32%)
  other arithmetic  46.8 us (21%)
  local copies, waits for them, and re-layouts  42.7 us (19%)
  matrix products  25.7 us (11%)
  waiting for transfers between devices  25 us (11%)
  starting transfers between devices  10.7 us (5%)
    scatter-add x2, other arithmetic, section_terms(): summed = jax.ops.segment_sum(products, target, num_segments=row_tiles)  42.4 us
    psum x1, blocking collectives, shards(): summed = lax.psum(partial_value, 'rep')  42.2 us
    all_to_all x1, blocking collectives, shards(): lax.all_to_all(rolled, 'blk', split_axis=0, concat_axis=0, tiled=True)  29.1 us
    all_to_all x1, waiting for transfers between devices, shards(): lax.all_to_all(pieces, 'blk', split_axis=0, concat_axis=0, tiled=True)  25 us
    dot_general x2, matrix products, section_terms(): jnp.einsum('kij,kjf->kif', tiles, pieces, preferred_element_type=jnp.floa...  23.6 us
    mul x2, local copies, waits for them, and re-layouts, section_terms(): products = products * live[:, None, None]  23.5 us
    gather x2, local copies, waits for them, and re-layouts, section_terms(): pieces = jnp.take(blocked, column, axis=0)  15.4 us
    all_to_all x1, starting transfers between devices, shards(): lax.all_to_all(pieces, 'blk', split_axis=0, concat_axis=0, tiled=True)  6.47 us
  transfers between devices with their start and end apart: 2, of which 1 were waited for; matrix products, arithmetic and copies ran while one was open for 15% of the time, Pallas kernels for 0%

commit v1 on v0

--- a/solution.py
+++ b/solution.py
@@ -41,7 +41,9 @@
             tile_place[0, section_index],
             tile_count[0, section_index],
         )
-    summed = lax.psum(partial_value, "rep")
+    summed = partial_value
+    for hop in (1, 2):
+        summed = summed + lax.ppermute(summed, "rep", [(dev, dev ^ hop) for dev in range(4)])
     aggregated = summed.astype(jnp.bfloat16)
     output = jnp.dot(aggregated, weight, preferred_element_type=jnp.float32) + bias
     return jnp.maximum(output, 0.0).astype(jnp.bfloat16)

time: 224 us -> 234 us (1.045)
  waiting for transfers between devices: 25 us -> 74.3 us
  blocking collectives: 71.3 us -> 29.1 us
  starting transfers between devices: 10.7 us -> 13.4 us
    ppermute x0 -> x2, waiting for transfers between devices: none -> 49.4 us  [shards(): lax.ppermute(summed, 'rep', [(dev, dev ^ hop) for dev in range(4)])]
    psum x1 -> x0, blocking collectives: 42.2 us -> none  [shards(): summed = lax.psum(partial_value, 'rep')]
    ppermute x0 -> x2, starting transfers between devices: none -> 2.68 us  [shards(): lax.ppermute(summed, 'rep', [(dev, dev ^ hop) for dev in range(4)])]
  transfers between devices with their start and end apart: 2 -> 4, of which waited for: 1 -> 3; matrix products, arithmetic and copies ran while one was open for 15% -> 14% of each run, Pallas kernels for 0% -> 0%
where the time goes in v1:
time: 234 us; the launch traced here: 231 us
  waiting for transfers between devices  74.3 us (32%)
  other arithmetic  45.7 us (20%)
  local copies, waits for them, and re-layouts  42.6 us (18%)
  blocking collectives  29.1 us (12%)
  matrix products  25.7 us (11%)
  starting transfers between devices  13.4 us (6%)
    ppermute x2, waiting for transfers between devices, shards(): lax.ppermute(summed, 'rep', [(dev, dev ^ hop) for dev in range(4)])  49.4 us
    scatter-add x2, other arithmetic, section_terms(): summed = jax.ops.segment_sum(products, target, num_segments=row_tiles)  42.4 us
    all_to_all x1, blocking collectives, shards(): lax.all_to_all(rolled, 'blk', split_axis=0, concat_axis=0, tiled=True)  29.1 us
    all_to_all x1, waiting for transfers between devices, shards(): lax.all_to_all(pieces, 'blk', split_axis=0, concat_axis=0, tiled=True)  25 us
    dot_general x2, matrix products, section_terms(): jnp.einsum('kij,kjf->kif', tiles, pieces, preferred_element_type=jnp.floa...  23.7 us
    mul x2, local copies, waits for them, and re-layouts, section_terms(): products = products * live[:, None, None]  23.5 us
    gather x2, local copies, waits for them, and re-layouts, section_terms(): pieces = jnp.take(blocked, column, axis=0)  15.4 us
    all_to_all x1, starting transfers between devices, shards(): lax.all_to_all(pieces, 'blk', split_axis=0, concat_axis=0, tiled=True)  6.47 us
  transfers between devices with their start and end apart: 4, of which 3 were waited for; matrix products, arithmetic and copies ran while one was open for 14% of the time, Pallas kernels for 0%

profile of v1, /device:TPU:1, one launch (start us, length us, event | category | flops | bytes accessed | tf_op | source)
XLA Modules:
  0.0 231.1 jit_solution(1260529867881614547)
XLA Ops:
  0.0 6.5 %all-to-all-start = ((bf16[8,512,128]{2,1,0:T(8,128)(2,1)}), bf16[8,512,128]{2,1,0:T(8,128)(2,1)S(1)}, u32[]{:S(2)}, u32[]{:S(2)}) async-start(bf16[8,512,128]{2,1,0:T(8,128)(2,1)} %bitcast.45), calls=%async_computation | async-start | bytes 2097152 | tf_op jit(solution)/shard_map/all_to_all | solution.py:32
  6.5 25.0 %all-to-all-done = bf16[8,512,128]{2,1,0:T(8,128)(2,1)S(1)} async-done(((bf16[8,512,128]{2,1,0:T(8,128)(2,1)}), bf16[8,512,128]{2,1,0:T(8,128)(2,1)S(1)}, u32[]{:S(2)}, u32[]{:S(2)}) %all-to-all-start) | async-done | bytes 1048608 | tf_op jit(solution)/shard_map/all_to_all | solution.py:32
  31.7 1.1 constant_dynamic-slice_fusion
  32.8 29.1 %all_to_all.15 = bf16[8,512,128]{2,1,0:T(8,128)(2,1)S(1)} all-to-all(bf16[8,512,128]{2,1,0:T(8,128)(2,1)S(1)} %get-tuple-element.11), channel_id=1, replica_groups=mesh['blk'=8,'rep'=4] {'blk'}, dimensions={0} | all-to-all | bytes 2097152 | tf_op jit(solution)/shard_map/all_to_all | solution.py:36
  61.9 4.3 %all-to-all-start.1 = ((bf16[8,512,128]{2,1,0:T(8,128)(2,1)}), bf16[8,512,128]{2,1,0:T(8,128)(2,1)S(1)}, u32[]{:S(2)}, u32[]{:S(2)}) async-start(bf16[8,512,128]{2,1,0:T(8,128)(2,1)} %get-tuple-element.12), calls=%async_computation.1 | async-start | bytes 2097152 | tf_op jit(solution)/shard_map/all_to_all | solution.py:36
  66.2 0.6 fusion.27
  66.9 0.6 compare_and_fusion
  67.5 0.6 compare_and_fusion.1
  68.2 7.7 %gather_fusion.1 = bf16[160,128,128]{2,1,0:T(8,128)(2,1)} fusion(bf16[32,128,128]{2,1,0:T(8,128)(2,1)S(1)} %bitcast.43, s32[1024]{0:T(1024)S(1)} %pad_clamp_fusion), kind=kCustom, calls=%fused_computation.1.clone | custom fusion | bytes 10486400 | tf_op jit(solution)/shard_map/jit(_take)/gather | solution.py:15
  75.9 11.8 %multiply_bitcast_fusion = f32[160,128,128]{1,2,0:T(8,128)} fusion(f32[160]{0:T(256)S(1)} %get-tuple-element.20, bf16[1,2,160,128,128]{4,3,2,1,0:T(8,128)(2,1)} %param.13, bf16[160,128,128]{2,1,0:T(8,128)(2,1)} %gather_fusion.1, pred[160]{0:T(512)(128)(4,1)S(1)} %get-tuple-element.6), kind=kOutput, calls=%fused_computation.4 | convolution fusion | flops 676331520 | bytes 20972320 | tf_op jit(solution)/shard_map/kij,kjf->kif/dot_general | solution.py:16
  87.7 11.7 %copy.12 = f32[160,128,128]{2,1,0:T(8,128)} copy(f32[160,128,128]{1,2,0:T(8,128)} %multiply_bitcast_fusion) | data formatting | bytes 20971520 | tf_op jit(solution)/shard_map/mul | solution.py:19
  99.4 7.7 %gather_fusion = bf16[160,128,128]{2,1,0:T(8,128)(2,1)} fusion(bf16[32,128,128]{2,1,0:T(8,128)(2,1)S(1)} %bitcast.42, s32[1024]{0:T(1024)S(1)} %pad_clamp_fusion.1), kind=kCustom, calls=%fused_computation.clone | custom fusion | bytes 10486400 | tf_op jit(solution)/shard_map/jit(_take)/gather | solution.py:15
  107.2 11.8 %multiply_bitcast_fusion.1 = f32[160,128,128]{1,2,0:T(8,128)} fusion(f32[160]{0:T(256)S(1)} %get-tuple-element.19, bf16[1,2,160,128,128]{4,3,2,1,0:T(8,128)(2,1)} %param.13, bf16[160,128,128]{2,1,0:T(8,128)(2,1)} %gather_fusion, pred[160]{0:T(512)(128)(4,1)S(1)} %get-tuple-element.9), kind=kOutput, calls=%fused_computation.5 | convolution fusion | flops 676331520 | bytes 20972320 | tf_op jit(solution)/shard_map/kij,kjf->kif/dot_general | solution.py:16
  119.0 11.7 %copy.10 = f32[160,128,128]{2,1,0:T(8,128)} copy(f32[160,128,128]{1,2,0:T(8,128)} %multiply_bitcast_fusion.1) | data formatting | bytes 20971520 | tf_op jit(solution)/shard_map/mul | solution.py:19
  131.0 21.2 %scatter_fusion.1 = f32[32,128,128]{2,1,0:T(8,128)S(1)} fusion(f32[32,128,128]{2,1,0:T(8,128)S(1)} %broadcast.127.clone.1, s32[160]{0:T(256)S(1)} %bitcast.47, f32[160,128,128]{2,1,0:T(8,128)} %copy.12), kind=kCustom, calls=%fused_computation.3 | custom fusion | flops 2621440 | bytes 31457920 | tf_op jit(solution)/shard_map/scatter-add | solution.py:20
  152.2 1.3 copy-done.1
  153.5 0.2 broadcast.127.clone
  153.7 21.2 %scatter_fusion = f32[32,128,128]{2,1,0:T(8,128)S(1)} fusion(f32[32,128,128]{2,1,0:T(8,128)S(1)} %broadcast.127.clone, s32[160]{0:T(256)S(1)} %bitcast.46, f32[160,128,128]{2,1,0:T(8,128)} %copy.10), kind=kCustom, calls=%fused_computation.2 | custom fusion | flops 2621440 | bytes 31457920 | tf_op jit(solution)/shard_map/scatter-add | solution.py:20
  174.9 1.8 add.70
  176.8 1.4 collective-permute-start
  178.1 3.8 %collective-permute-done = f32[4096,128]{1,0:T(8,128)S(1)} collective-permute-done((f32[4096,128]{1,0:T(8,128)S(1)}, f32[4096,128]{1,0:T(8,128)S(1)}, u32[]{:S(2)}, u32[]{:S(2)}) %collective-permute-start) | collective-permute-done | bytes 2097184 | tf_op jit(solution)/shard_map/ppermute | solution.py:46
  182.1 1.3 collective-permute-start.1
  183.4 45.6 %collective-permute-done.1 = f32[4096,128]{1,0:T(8,128)S(1)} collective-permute-done((f32[4096,128]{1,0:T(8,128)S(1)}, f32[4096,128]{1,0:T(8,128)S(1)}, u32[]{:S(2)}, u32[]{:S(2)}) %collective-permute-start.1) | collective-permute-done | bytes 2097184 | tf_op jit(solution)/shard_map/ppermute | solution.py:46
  229.0 2.0 fusion.11
  (18 shorter events, 0.7 us)
Async XLA Ops:
  0.0 229.0 %copy-start = (bf16[128,256]{1,0:T(8,128)(2,1)S(1)}, bf16[128,256]{1,0:T(8,128)(2,1)}, u32[]{:S(2)}) copy-start(bf16[128,256]{1,0:T(8,128)(2,1)} %param.11) | copy-start | bytes 196612
  0.0 31.4 %all-to-all-start = ((bf16[8,512,128]{2,1,0:T(8,128)(2,1)}), bf16[8,512,128]{2,1,0:T(8,128)(2,1)S(1)}, u32[]{:S(2)}, u32[]{:S(2)}) async-start(bf16[8,512,128]{2,1,0:T(8,128)(2,1)} %bitcast.45), calls=%async_computation | async-start | bytes 2097152 | tf_op jit(solution)/shard_map/all_to_all | solution.py:32
  31.5 34.7 %copy-start.2 = (s32[1,2,160]{2,1,0:T(2,128)S(1)}, s32[1,2,160]{2,1,0:T(2,128)}, u32[]{:S(2)}) copy-start(s32[1,2,160]{2,1,0:T(2,128)} %param.14) | copy-start | bytes 3844
  31.5 34.7 %copy-start.3 = (s32[1,2]{1,0:T(1,128)S(1)}, s32[1,2]{1,0:T(1,128)}, u32[]{:S(2)}) copy-start(s32[1,2]{1,0:T(1,128)} %param.15) | copy-start | bytes 28
  61.9 37.5 %all-to-all-start.1 = ((bf16[8,512,128]{2,1,0:T(8,128)(2,1)}), bf16[8,512,128]{2,1,0:T(8,128)(2,1)S(1)}, u32[]{:S(2)}, u32[]{:S(2)}) async-start(bf16[8,512,128]{2,1,0:T(8,128)(2,1)} %get-tuple-element.12), calls=%async_computation.1 | async-start | bytes 2097152 | tf_op jit(solution)/shard_map/all_to_all | solution.py:36
  152.1 1.3 copy-start.1
  174.9 54.1 %copy-start.4 = (f32[256]{0:T(256)S(1)}, f32[256]{0:T(256)}, u32[]{:S(2)}) copy-start(f32[256]{0:T(256)} %param.12) | copy-start | bytes 3076
  176.8 5.2 %collective-permute-start = (f32[4096,128]{1,0:T(8,128)S(1)}, f32[4096,128]{1,0:T(8,128)S(1)}, u32[]{:S(2)}, u32[]{:S(2)}) collective-permute-start(f32[4096,128]{1,0:T(8,128)S(1)} %bitcast.44), channel_id=1, source_target_pairs={{0,1},{1,0},{2,3},{3,2},{4,5},{5,4},{6,7},{7,6},{8,9},{9,8},{10,11... | collective-permute-start | bytes 6291464 | tf_op jit(solution)/shard_map/ppermute | solution.py:46
  182.1 46.9 %collective-permute-start.1 = (f32[4096,128]{1,0:T(8,128)S(1)}, f32[4096,128]{1,0:T(8,128)S(1)}, u32[]{:S(2)}, u32[]{:S(2)}) collective-permute-start(f32[4096,128]{1,0:T(8,128)S(1)} %bitcast_add_fusion), channel_id=1, source_target_pairs={{0,2},{1,3},{2,0},{3,1},{4,6},{5,7},{6,4},{7,5},{8,10},{9,11},{10,... | collective-permute-start | bytes 6291464 | tf_op jit(solution)/shard_map/ppermute | solution.py:46
